TPU v7x, 32 devices: a whole 2x2x4 slice. The times are simulated.
32 devices in a mesh: dp: 8 (over y, x, core), tensor: 4 (over z).
Axes of the slice: x: 2, y: 2, z: 4, core: 2. Of those that a mesh axis runs over, the one named last changes fastest.
Arguments:
- wq_flat: bfloat16 [8192, 4096], P(('dp', 'tensor')), may hold values from -0.125 to 0.125
- hidden: bfloat16 [4, 16, 8192], P(None, 'dp'), may hold values from -6 to 6
- cache: bfloat16 [16, 4, 8192, 256], P('dp', None, 'tensor'), may hold values from -300 to 300
- new_kv: bfloat16 [4, 16, 4, 256], P(None, 'dp'), may hold values from -6 to 6
- lengths: int32 [16], P('dp'), may hold values from 1 to 8192, as said below
Outputs:
- attended: bfloat16 [4, 16, 4096], P(None, 'dp', 'tensor')
Inputs may be any that keep to these rules, and one draw needn't show every extreme that they name: `lengths`: every sequence has at least one cached position; in every draw some sequence has exactly 8192.
All inputs are finite; a program needn't handle non-finite values.
Results may differ from a plain program's by a relative error of at most 0.03.
Values may be sent and summed in bfloat16 or wider, within the bound.
A program may use at most 64 MiB of HBM per device.

v0:
```python
import jax
import jax.numpy as jnp
from jax import lax
from jax.sharding import PartitionSpec as P

QH = 32
HD = 128


def merged(shard, axis, combine):
    everything = jax.tree.map(lambda part: lax.all_gather(part, axis), shard)
    initial = jax.tree.map(lambda part: part[0], everything)

    def step(k, so_far):
        return combine(so_far, jax.tree.map(lambda part: part[k], everything))

    return lax.fori_loop(1, lax.axis_size(axis), step, initial)


def combine_parts(first, second):
    best = jnp.maximum(first[0], second[0])
    scale_one = jnp.exp(first[0] - best)
    scale_two = jnp.exp(second[0] - best)
    total = first[1] * scale_one + second[1] * scale_two
    accum = first[2] * scale_one[..., None] + second[2] * scale_two[..., None]
    return (best, total, accum)


def body(wq_flat, hidden, cache, new_kv, lengths):
    n_tensor = lax.axis_size("tensor")
    n_replica = lax.axis_size("dp")
    rank = lax.axis_index("tensor")
    steps, seq_dev, width = hidden.shape
    kv_heads = cache.shape[1]
    ctx_dev = cache.shape[2]
    group = QH // kv_heads
    heads_dev = QH // n_tensor
    scale = 1.0 / HD**0.5
    rows = steps * seq_dev
    flat_rows = hidden.reshape(rows, width)
    shard_rows = wq_flat.shape[0]
    blocks = flat_rows.reshape(rows, n_replica, n_tensor, shard_rows)
    picked = lax.dynamic_index_in_dim(blocks, rank, 2, keepdims=False).reshape(
        rows, n_replica * shard_rows
    )
    partial_value = jnp.dot(
        picked,
        lax.all_gather(wq_flat, "dp", axis=0, tiled=True),
        preferred_element_type=jnp.float32,
    )
    query_all = lax.psum(partial_value, "tensor").astype(jnp.bfloat16)
    query_own = lax.dynamic_slice_in_dim(query_all, rank * heads_dev * HD, heads_dev * HD, 1)
    queries = query_all.reshape(steps, seq_dev, kv_heads, group, HD)
    keys = cache[..., :HD]
    values = cache[..., HD:]
    scores = (
        jnp.einsum("tsgjd,sgcd->gjtsc", queries, keys, preferred_element_type=jnp.float32) * scale
    )
    positions = rank * ctx_dev + jnp.arange(ctx_dev)
    valid = (positions[None, :] < lengths[:, None])[None, None, None, :, :]
    masked = jnp.where(valid, scores, -1e30)
    local_max = jnp.max(masked, axis=-1)
    weights = jnp.where(valid, jnp.exp(masked - local_max[..., None]), 0.0)
    local_total = jnp.sum(weights, axis=-1)
    local_acc = jnp.einsum(
        "gjtsc,sgcd->gjtsd",
        weights.astype(jnp.bfloat16),
        values,
        preferred_element_type=jnp.float32,
    )
    local_max = local_max.reshape(QH, steps, seq_dev)
    local_total = local_total.reshape(QH, steps, seq_dev)
    local_acc = local_acc.reshape(QH, steps, seq_dev, HD)
    best, denom, accum = merged((local_max, local_total, local_acc), "tensor", combine_parts)
    best = lax.dynamic_slice_in_dim(best, rank * heads_dev, heads_dev, 0)
    denom = lax.dynamic_slice_in_dim(denom, rank * heads_dev, heads_dev, 0)
    accum = lax.dynamic_slice_in_dim(accum, rank * heads_dev, heads_dev, 0)
    kv_index = rank * heads_dev // group
    fresh = lax.dynamic_slice_in_dim(new_kv, kv_index, 1, 2)[:, :, 0, :]
    own_q = query_own.reshape(steps, seq_dev, heads_dev, HD)
    new_scores = (
        jnp.einsum("tsjd,usd->jtsu", own_q, fresh[..., :HD], preferred_element_type=jnp.float32)
        * scale
    )
    causal = (jnp.arange(steps)[:, None] >= jnp.arange(steps)[None, :])[None, :, None, :]
    new_masked = jnp.where(causal, new_scores, -1e30)
    top = jnp.maximum(best, jnp.max(new_masked, axis=-1))
    old_scale = jnp.exp(best - top)
    new_weights = jnp.where(causal, jnp.exp(new_masked - top[..., None]), 0.0)
    denom = denom * old_scale + jnp.sum(new_weights, axis=-1)
    accum = accum * old_scale[..., None] + jnp.einsum(
        "jtsu,usd->jtsd",
        new_weights.astype(jnp.bfloat16),
        fresh[..., HD:],
        preferred_element_type=jnp.float32,
    )
    result = accum / denom[..., None]
    return result.transpose(1, 2, 0, 3).reshape(steps, seq_dev, heads_dev * HD).astype(jnp.bfloat16)


def solution(mesh):
    placed = (
        P(("dp", "tensor"), None),
        P(None, "dp", None),
        P("dp", None, "tensor", None),
        P(None, "dp", None, None),
        P("dp"),
    )
    return jax.shard_map(
        body, mesh=mesh, in_specs=placed, out_specs=P(None, "dp", "tensor"), check_vma=False
    )
```

profile of v0, /device:TPU:0, one launch (start us, length us, event | category | flops | bytes accessed | tf_op | source)
XLA Modules:
  0.0 189.2 jit_solution(12184188657150206391)
XLA Ops:
  6.5 0.7 all-gather.2.cloned.1.call-update
  7.3 0.2 copy-done.2
  7.5 0.1 reshape_reshape.3
  7.6 0.2 dynamic-slice_reduce_fusion
  8.0 5.8 %fusion.34 = (bf16[2,4,2048,128]{3,2,1,0:T(8,128)(2,1)}, bf16[2,4,2048,128]{3,2,1,0:T(8,128)(2,1)}) fusion(bf16[2,4,2048,256]{3,2,1,0:T(8,128)(2,1)} %param.9), kind=kLoop, calls=%fused_computation.61 | loop fusion | bytes 16777216 | tf_op jit(solution)/shard_map/slice | solution.py:55
  13.7 88.0 %all-gather.2.cloned.1.call-done = bf16[2048,4096]{1,0:T(8,128)(2,1)} async-done(((bf16[256,4096]{1,0:T(8,128)(2,1)}), bf16[2048,4096]{1,0:T(8,128)(2,1)}) %all-gather.2.cloned.1.call-update) | async-done | bytes 16777232 | tf_op jit(solution)/shard_map/all_gather | solution.py:48
  101.7 8.0 %fusion.37 = f32[8,4096]{1,0:T(8,128)S(1)} fusion(bf16[8,2048]{1,0:T(8,128)(2,1)S(1)} %bitcast.110, bf16[2048,4096]{1,0:T(8,128)(2,1)} %all-gather.2.cloned.1.call-done), kind=kOutput, calls=%fused_computation.64 | convolution fusion | flops 134217728 | bytes 16941056 | tf_op jit(solution)/shard_map/dot_general | solution.py:46
  109.7 21.2 %all-reduce.1 = bf16[8,4096]{1,0:T(8,128)(2,1)S(1)} all-reduce(f32[8,4096]{1,0:T(8,128)S(1)} %fusion.37), channel_id=1, replica_groups=mesh['dp'=8,'tensor'=4] {'tensor'}, use_global_device_ids=true, to_apply=%region_0.1 | all-reduce | flops 32768 | bytes 196608 | tf_op jit(solution)/shard_map/psum | solution.py:51
  130.9 3.9 %fusion.35 = (f32[4,8,4,2]{1,2,3,0:T(4,128)S(1)}, f32[4,8,4,2,2048]{4,1,2,3,0:T(8,128)S(1)}) fusion(bf16[2,4,2048,128]{3,2,1,0:T(8,128)(2,1)} %get-tuple-element.230, bf16[4,2,4,8,128]{4,3,2,1,0:T(8,128)(2,1)S(1)} %bitcast.109, pred[2,2048]{1,0:T(4,128)(4,1)S(1)} %broadcast_compare_fusion), kind=kOutput, calls=%fused_computation.62 | convolution fusion | flops 135790336 | bytes 6362112 | tf_op jit(solution)/shard_map/tsgjd,sgcd->gjtsc/dot_general | solution.py:57
  134.9 0.5 fusion.11
  135.4 0.8 fusion.12
  136.2 14.7 %all_gather.15 = f32[4,32,4,2,128]{4,1,3,2,0:T(8,128)S(1)} all-gather(f32[1,32,4,2,128]{4,1,3,2,0:T(8,128)S(1)} %bitcast.107), channel_id=1, replica_groups=mesh['dp'=8,'tensor'=4] {'tensor'}, dimensions={0}, use_global_device_ids=true | all-gather | bytes 655360 | tf_op jit(solution)/shard_map/all_gather | solution.py:11
  150.9 0.1 copy.67
  151.0 0.1 reshape.67
  151.1 13.2 %all_gather.14 = f32[4,32,4,2]{1,2,3,0:T(4,128)S(1)} all-gather(f32[1,32,4,2]{1,2,3,0:T(4,128)S(1)} %reshape.67), channel_id=1, replica_groups=mesh['dp'=8,'tensor'=4] {'tensor'}, dimensions={0}, use_global_device_ids=true | all-gather | bytes 5120 | tf_op jit(solution)/shard_map/all_gather | solution.py:11
  164.3 0.1 all_gather_reshape.9
  164.4 13.2 %all_gather.13 = f32[4,32,4,2]{1,2,3,0:T(4,128)S(1)} all-gather(f32[1,32,4,2]{1,2,3,0:T(4,128)S(1)} %all_gather_reshape.9), channel_id=1, replica_groups=mesh['dp'=8,'tensor'=4] {'tensor'}, dimensions={0}, use_global_device_ids=true | all-gather | bytes 5120 | tf_op jit(solution)/shard_map/all_gather | solution.py:11
  177.6 3.3 %while.19 = (s32[]{:T(128)}, f32[32,4,2]{0,2,1:T(2,128)S(1)}, f32[32,4,2]{0,2,1:T(2,128)S(1)}, f32[32,4,2,128]{3,2,1,0:T(2,128)S(1)}, f32[4,32,4,2]{1,2,3,0:T(4,...) while((s32[]{:T(128)}, f32[32,4,2]{0,2,1:T(2,128)S(1)}, ...), condition=%wide.region_4.5_spmd, body=%wide.region_3.4_spmd.sunk | while | flops 99845 | bytes 673943 | solution.py:17
  177.7 0.1 copy.141
  177.8 0.1 copy.142
  177.9 0.8 fusion.43
  178.8 0.1 copy.141
  178.9 0.1 copy.142
  179.0 0.8 fusion.43
  179.9 0.1 copy.141
  180.0 0.1 copy.142
  180.1 0.8 fusion.43
  181.0 0.2 fusion.36
  181.3 0.1 fusion.25
  181.4 0.1 multiply_add_fusion
  181.5 0.3 fusion.16
  181.8 0.6 copy.76
  (39 shorter events, 0.5 us)
Async XLA Ops:
  6.5 1.3 copy-start
  6.5 0.9 copy-start.2
  6.5 1.3 copy-start.3
  6.5 95.2 %all-gather.2.cloned.1.call-start = ((), (), s32[]{:S(2)}) async-start(), calls=%async_computation | async-start | bytes 18874368 | tf_op jit(solution)/shard_map/all_gather | solution.py:48
  130.9 4.4 %copy-start.1 = (bf16[2,4,2048,128]{3,2,1,0:T(8,128)(2,1)S(1)}, bf16[2,4,2048,128]{3,2,1,0:T(8,128)(2,1)}, u32[]{:S(2)}) copy-start(bf16[2,4,2048,128]{3,2,1,0:T(8,128)(2,1)} %get-tuple-element.229) | copy-start | bytes 12582916
Sparse Core Ops, SparseCore 0:
  9.2 92.4 all-gather.1
where the time goes:
time: 189 us
  waiting for transfers between devices  88.7 us (47%)
  blocking collectives  62.2 us (33%)
  between operations  13.6 us (7%)
  matrix products  13.2 us (7%)
  local copies, waits for them, and re-layouts  8.06 us (4%)
  other arithmetic  3.33 us (2%)
    all_gather x1, waiting for transfers between devices, body(): lax.all_gather(wq_flat, 'dp', axis=0, tiled=True)  88 us
    all_gather x3, blocking collectives, merged(): everything = jax.tree.map(lambda part: lax.all_gather(part, axis), shard)  41.1 us
    psum x1, blocking collectives, body(): query_all = lax.psum(partial_value, 'tensor').astype(jnp.bfloat16)  21.2 us
    dot_general x1, matrix products, body(): jnp.dot(picked, lax.all_gather(wq_flat, 'dp', axis=0, tiled=True), prefer...  8.04 us
    slice x1, local copies, waits for them, and re-layouts, body(): values = cache[..., HD:]  5.76 us
    dot_general x1, matrix products, body(): jnp.einsum('tsgjd,sgcd->gjtsc', queries, keys, preferred_element_type=jnp...  3.89 us
  transfers between devices with their start and end apart: 1, of which 1 were waited for; matrix products, arithmetic and copies ran while one was open for 3% of the time, Pallas kernels for 0%

commit v1 on v0

v1 whole, which is shorter than its diff:
```python
import functools

import jax
import jax.numpy as jnp
from jax import lax
from jax.experimental import pallas as pl
from jax.experimental.pallas import tpu as pltpu
from jax.sharding import PartitionSpec as P

QH = 32
HD = 128
MESH = pl.DeviceIdType.MESH
NEG = -1e30


def kernel(
    n,
    nt,
    lengths,
    hid,
    fresh,
    wq,
    cache,
    out,
    wq_own,
    wq_other,
    kv,
    xg,
    yown,
    ysend,
    yrecv,
    psend,
    precv,
    zsend,
    zrecv,
    qsend,
    qbuf,
    q_sc,
    acc_sc,
    asend,
    arecv,
    m_sc,
    l_sc,
    ssend,
    srecv,
    sem_w,
    sem_kv,
    sx_s,
    sx_r,
    sy_s,
    sy_r,
    sp_s,
    sp_r,
    sz_s,
    sz_r,
    sq_s,
    sq_r,
    sa_s,
    sa_r,
    ss_s,
    ss_r,
):
    d = lax.axis_index("dp")
    t = lax.axis_index("tensor")
    core = lax.rem(d, 2)
    chip = d // 2
    chips = n // 2
    mate = d + 1 - 2 * core
    rows = hid.shape[1]
    half = wq_own.shape[1]
    seqs, kvh, ctx, _ = kv.shape
    heads = QH // nt
    group = QH // kvh
    scale = 1.0 / HD**0.5

    load_other = pltpu.make_async_copy(
        wq.at[:, pl.ds(pl.multiple_of((1 - core) * half, half), half)], wq_other, sem_w.at[0]
    )
    load_own = pltpu.make_async_copy(
        wq.at[:, pl.ds(pl.multiple_of(core * half, half), half)], wq_own, sem_w.at[1]
    )
    load_other.start()
    load_own.start()
    load_kv = [
        [pltpu.make_async_copy(cache.at[s, g], kv.at[s, g], sem_kv.at[s, g]) for g in range(kvh)]
        for s in range(seqs)
    ]
    for g in range(kvh):
        for s in range(seqs):
            load_kv[s][g].start()

    barrier = pltpu.get_barrier_semaphore()

    @pl.loop(1, n)
    def _(k):
        pl.semaphore_signal(
            barrier, inc=1, device_id=(lax.rem(d + k, n), t), device_id_type=MESH
        )

    @pl.loop(1, nt)
    def _(k):
        peer = lax.rem(t + k, nt)
        pl.semaphore_signal(barrier, inc=1, device_id=(d, peer), device_id_type=MESH)
        pl.semaphore_signal(barrier, inc=1, device_id=(mate, peer), device_id_type=MESH)

    pl.semaphore_wait(barrier, n - 1 + 2 * (nt - 1))

    def x_copy(k, slot, peer, source):
        return pltpu.make_async_remote_copy(
            src_ref=hid.at[peer],
            dst_ref=xg.at[slot],
            send_sem=sx_s.at[k],
            recv_sem=sx_r.at[source],
            device_id=(peer, t),
            device_id_type=MESH,
        )

    @pl.loop(1, n)
    def _(k):
        x_copy(k, d, lax.rem(d + k, n), d).start()

    xg[d] = hid[d]
    load_other.wait()
    load_own.wait()

    @pl.loop(1, n)
    def _(k):
        peer = lax.rem(d + k, n)
        x_copy(k, peer, peer, peer).wait_recv()

    x = xg[...].reshape(n * rows, xg.shape[2]).astype(jnp.bfloat16)

    psend[...] = (
        jnp.dot(x, wq_other[...], preferred_element_type=jnp.float32)
        .astype(jnp.bfloat16)
        .reshape(chips, 2 * rows, half)
    )

    def p_copy(p):
        return pltpu.make_async_remote_copy(
            src_ref=psend.at[p],
            dst_ref=precv.at[p],
            send_sem=sp_s.at[p],
            recv_sem=sp_r.at[p],
            device_id=(mate, t),
            device_id_type=MESH,
        )

    def order(k):
        return lax.rem(chip + chips - k, chips)

    @pl.loop(1, chips + 1)
    def _(k):
        p_copy(order(k)).start()

    yown[...] = jnp.dot(x, wq_own[...], preferred_element_type=jnp.float32).reshape(
        chips, 2 * rows, half
    )

    def y_copy(k, slot, peer, source):
        return pltpu.make_async_remote_copy(
            src_ref=ysend.at[peer],
            dst_ref=yrecv.at[slot],
            send_sem=sy_s.at[k],
            recv_sem=sy_r.at[source],
            device_id=(2 * peer + core, t),
            device_id_type=MESH,
        )

    @pl.loop(1, chips)
    def _(k):
        p = order(k)
        p_copy(p).wait_recv()
        ysend[p] = (yown[p] + precv[p].astype(jnp.float32)).astype(jnp.bfloat16)
        y_copy(k, chip, p, chip).start()

    p_copy(chip).wait_recv()
    z0 = yown[chip] + precv[chip].astype(jnp.float32)

    def y_add(k, z):
        p = order(k)
        y_copy(k, p, p, p).wait_recv()
        return z + yrecv[p].astype(jnp.float32)

    z = lax.fori_loop(1, chips, y_add, z0)

    part = half // nt
    for j in range(nt):
        zsend[j] = z[:, j * part : (j + 1) * part].astype(zsend.dtype)

    def z_copy(k, slot, peer, source):
        return pltpu.make_async_remote_copy(
            src_ref=zsend.at[peer],
            dst_ref=zrecv.at[slot],
            send_sem=sz_s.at[k],
            recv_sem=sz_r.at[source],
            device_id=(d, peer),
            device_id_type=MESH,
        )

    @pl.loop(1, nt)
    def _(k):
        z_copy(k, t, lax.rem(t + k, nt), t).start()

    def z_add(k, total):
        peer = lax.rem(t + k, nt)
        z_copy(k, peer, peer, peer).wait_recv()
        return total + zrecv[peer].astype(jnp.float32)

    piece = lax.fori_loop(1, nt, z_add, zsend[t].astype(jnp.float32))
    for c in range(2):
        qsend[c] = piece[c * rows : (c + 1) * rows].astype(jnp.bfloat16)

    def q_copy(k, which, peer_core, peer, slot):
        return pltpu.make_async_remote_copy(
            src_ref=qsend.at[peer_core],
            dst_ref=qbuf.at[slot],
            send_sem=sq_s.at[k, which],
            recv_sem=sq_r.at[slot],
            device_id=(2 * chip + peer_core, peer),
            device_id_type=MESH,
        )

    mine = core * nt + t

    @pl.loop(1, nt)
    def _(k):
        peer = lax.rem(t + k, nt)
        q_copy(k, 0, core, peer, mine).start()
        q_copy(k, 1, 1 - core, peer, mine).start()

    q_copy(0, 1, 1 - core, t, mine).start()
    qbuf[mine] = qsend[core]
    q_copy(0, 1, 1 - core, t, (1 - core) * nt + t).wait_recv()

    @pl.loop(1, nt)
    def _(k):
        peer = lax.rem(t + k, nt)
        q_copy(k, 0, core, peer, core * nt + peer).wait_recv()
        q_copy(k, 1, core, peer, (1 - core) * nt + peer).wait_recv()

    heads_slot = part // HD
    for slot in range(2 * nt):
        block = qbuf[slot].astype(jnp.float32)
        for j in range(heads_slot):
            h = slot * heads_slot + j
            q_sc[h * rows : (h + 1) * rows, :] = block[:, j * HD : (j + 1) * HD]

    steps = rows // seqs
    band = group * rows
    position = t * ctx + lax.broadcasted_iota(jnp.int32, (1, ctx), 1)
    owned = heads * rows

    def a_copy(k, slot, peer, source):
        return pltpu.make_async_remote_copy(
            src_ref=asend.at[peer],
            dst_ref=arecv.at[slot],
            send_sem=sa_s.at[k],
            recv_sem=sa_r.at[source],
            device_id=(d, peer),
            device_id_type=MESH,
        )

    def s_copy(k, slot, peer, source):
        return pltpu.make_async_remote_copy(
            src_ref=ssend.at[peer],
            dst_ref=srecv.at[slot],
            send_sem=ss_s.at[k],
            recv_sem=ss_r.at[source],
            device_id=(d, peer),
            device_id_type=MESH,
        )

    for g in range(kvh):
        for s in range(seqs):
            load_kv[s][g].wait()
            span = pl.ds(g * band + s, group * steps, stride=seqs)
            q = q_sc[span, :].astype(jnp.bfloat16)
            scores = (
                lax.dot_general(
                    q,
                    kv[s, g, :, :HD],
                    (((1,), (1,)), ((), ())),
                    preferred_element_type=jnp.float32,
                )
                * scale
            )
            valid = position < lengths[s]
            masked = jnp.where(valid, scores, NEG)
            best = jnp.max(masked, axis=-1, keepdims=True)
            weights = jnp.where(valid, jnp.exp(masked - best), 0.0)
            total = jnp.sum(weights, axis=-1, keepdims=True)
            acc = jnp.dot(
                weights.astype(jnp.bfloat16), kv[s, g, :, HD:], preferred_element_type=jnp.float32
            )
            acc_sc[span, :] = acc
            m_sc[span, :] = jnp.broadcast_to(best, acc.shape)
            l_sc[span, :] = jnp.broadcast_to(total, acc.shape)

    eye = lax.broadcasted_iota(jnp.int32, (owned, HD), 0) == lax.broadcasted_iota(
        jnp.int32, (owned, HD), 1
    )
    for j in range(nt):
        window = slice(j * owned, (j + 1) * owned)
        asend[j] = acc_sc[window, :].astype(asend.dtype)
        ssend[j, 0:1, :] = jnp.sum(jnp.where(eye, m_sc[window, :], 0.0), axis=0, keepdims=True)
        ssend[j, 1:2, :] = jnp.sum(jnp.where(eye, l_sc[window, :], 0.0), axis=0, keepdims=True)

    @pl.loop(1, nt)
    def _(k):
        peer = lax.rem(t + k, nt)
        a_copy(k, t, peer, t).start()
        s_copy(k, t, peer, t).start()

    own = pl.ds(pl.multiple_of(t * owned, owned), owned)
    q_own = q_sc[own, :].astype(jnp.bfloat16)
    new_scores = (
        lax.dot_general(
            q_own, fresh[:, :HD], (((1,), (1,)), ((), ())), preferred_element_type=jnp.float32
        )
        * scale
    )
    row = lax.broadcasted_iota(jnp.int32, new_scores.shape, 0)
    col = lax.broadcasted_iota(jnp.int32, new_scores.shape, 1)
    row_seq = lax.rem(row, seqs)
    row_step = lax.rem(row, rows) // seqs
    causal = (row_seq == lax.rem(col, seqs)) & (row_step >= col // seqs)
    new_masked = jnp.where(causal, new_scores, NEG)
    top = jnp.max(new_masked, axis=-1, keepdims=True)
    new_weights = jnp.where(causal, jnp.exp(new_masked - top), 0.0)
    denom = jnp.sum(new_weights, axis=-1, keepdims=True)
    accum = jnp.dot(
        new_weights.astype(jnp.bfloat16), fresh[:, HD:], preferred_element_type=jnp.float32
    )

    def join(state, best, total, acc):
        top, denom, accum = state
        peak = jnp.maximum(top, best)
        left = jnp.exp(top - peak)
        right = jnp.exp(best - peak)
        return peak, denom * left + total * right, accum * left + acc * right

    state = join((top, denom, accum), m_sc[own, :][:, :1], l_sc[own, :][:, :1], acc_sc[own, :])

    def a_join(k, state):
        peer = lax.rem(t + k, nt)
        a_copy(k, peer, peer, peer).wait_recv()
        s_copy(k, peer, peer, peer).wait_recv()
        stats = srecv[peer]
        best = jnp.sum(jnp.where(eye, stats[0:1, :], 0.0), axis=1, keepdims=True)
        total = jnp.sum(jnp.where(eye, stats[1:2, :], 0.0), axis=1, keepdims=True)
        return join(state, best, total, arecv[peer].astype(jnp.float32))

    top, denom, accum = lax.fori_loop(1, nt, a_join, state)
    result = accum / denom
    for j in range(heads):
        out[:, j * HD : (j + 1) * HD] = result[j * rows : (j + 1) * rows].astype(out.dtype)

    @pl.loop(1, n)
    def _(k):
        x_copy(k, d, lax.rem(d + k, n), d).wait_send()

    @pl.loop(1, chips + 1)
    def _(k):
        p_copy(order(k)).wait_send()

    @pl.loop(1, chips)
    def _(k):
        y_copy(k, chip, order(k), chip).wait_send()

    q_copy(0, 1, 1 - core, t, mine).wait_send()

    @pl.loop(1, nt)
    def _(k):
        peer = lax.rem(t + k, nt)
        z_copy(k, t, peer, t).wait_send()
        q_copy(k, 0, core, peer, mine).wait_send()
        q_copy(k, 1, 1 - core, peer, mine).wait_send()
        a_copy(k, t, peer, t).wait_send()
        s_copy(k, t, peer, t).wait_send()


def body(wq_flat, hidden, cache, new_kv, lengths):
    nt = lax.axis_size("tensor")
    n = lax.axis_size("dp")
    t = lax.axis_index("tensor")
    steps, seqs, width = hidden.shape
    rows = steps * seqs
    depth, columns = wq_flat.shape
    kvh, ctx = cache.shape[1], cache.shape[2]
    half = columns // 2
    part = half // nt
    heads = QH // nt
    group = QH // kvh
    owned = heads * rows
    chips = n // 2
    blocks = hidden.reshape(rows, n, nt, depth)
    hid = lax.dynamic_index_in_dim(blocks, t, 2, keepdims=False).astype(jnp.float32)
    hid = hid.transpose(1, 0, 2)
    fresh = lax.dynamic_index_in_dim(new_kv, t * heads // group, 2, keepdims=False)
    fresh = jnp.pad(fresh.reshape(rows, 2 * HD), ((0, HD - rows), (0, 0)))
    bf16, f32 = jnp.bfloat16, jnp.float32
    dma = pltpu.SemaphoreType.DMA
    vmem = pl.BlockSpec(memory_space=pltpu.VMEM)
    anywhere = pl.BlockSpec(memory_space=pl.ANY)
    result = pl.pallas_call(
        functools.partial(kernel, n, nt),
        out_shape=jax.ShapeDtypeStruct((rows, heads * HD), bf16),
        in_specs=[pl.BlockSpec(memory_space=pltpu.SMEM), vmem, vmem, anywhere, anywhere],
        out_specs=vmem,
        scratch_shapes=[
            pltpu.VMEM((depth, half), bf16),
            pltpu.VMEM((depth, half), bf16),
            pltpu.VMEM(cache.shape, bf16),
            pltpu.VMEM((n, rows, depth), f32),
            pltpu.VMEM((chips, 2 * rows, half), f32),
            pltpu.VMEM((chips, 2 * rows, half), bf16),
            pltpu.VMEM((chips, 2 * rows, half), bf16),
            pltpu.VMEM((chips, 2 * rows, half), bf16),
            pltpu.VMEM((chips, 2 * rows, half), bf16),
            pltpu.VMEM((nt, 2 * rows, part), bf16),
            pltpu.VMEM((nt, 2 * rows, part), bf16),
            pltpu.VMEM((2, rows, part), bf16),
            pltpu.VMEM((2 * nt, rows, part), bf16),
            pltpu.VMEM((QH * rows, HD), f32),
            pltpu.VMEM((QH * rows, HD), f32),
            pltpu.VMEM((nt, owned, HD), bf16),
            pltpu.VMEM((nt, owned, HD), bf16),
            pltpu.VMEM((QH * rows, HD), f32),
            pltpu.VMEM((QH * rows, HD), f32),
            pltpu.VMEM((nt, 8, HD), f32),
            pltpu.VMEM((nt, 8, HD), f32),
            dma((2,)),
            dma((seqs, kvh)),
            dma((n,)),
            dma((n,)),
            dma((chips,)),
            dma((chips,)),
            dma((chips,)),
            dma((chips,)),
            dma((nt,)),
            dma((nt,)),
            dma((nt, 2)),
            dma((2 * nt,)),
            dma((nt,)),
            dma((nt,)),
            dma((nt,)),
            dma((nt,)),
        ],
        compiler_params=pltpu.CompilerParams(collective_id=0, has_side_effects=True),
    )(lengths, hid, fresh, wq_flat, cache)
    return result.reshape(steps, seqs, heads * HD)


def solution(mesh):
    placed = (
        P(("dp", "tensor"), None),
        P(None, "dp", None),
        P("dp", None, "tensor", None),
        P(None, "dp", None, None),
        P("dp"),
    )
    return jax.shard_map(
        body, mesh=mesh, in_specs=placed, out_specs=P(None, "dp", "tensor"), check_vma=False
    )
```

time: 189 us -> 38.1 us (0.20)
  waiting for transfers between devices: 88.7 us -> 0 us
  blocking collectives: 62.2 us -> 0 us
  Pallas kernels: 0 us -> 34.1 us
  between operations: 13.6 us -> 0.03 us
  matrix products: 13.2 us -> 0 us
  local copies, waits for them, and re-layouts: 8.06 us -> 3.12 us
  other arithmetic: 3.33 us -> 0.64 us
    all_gather x1 -> x0, waiting for transfers between devices: 88 us -> none  [body(): lax.all_gather(wq_flat, 'dp', axis=0, tiled=True)]
    all_gather x3 -> x0, blocking collectives: 41.1 us -> none  [merged(): everything = jax.tree.map(lambda part: lax.all_gather(part, axis), shard)]
    pallas_call x0 -> x1, Pallas kernels: none -> 34.1 us  [body(): pl.pallas_call(functools.partial(kernel, n, nt), out_shape=jax.ShapeDtype...]
    psum x1 -> x0, blocking collectives: 21.2 us -> none  [body(): query_all = lax.psum(partial_value, 'tensor').astype(jnp.bfloat16)]
    dot_general x5 -> x0, matrix products: 13.2 us -> none  [the longest x1 8.04 us: body(): jnp.dot(picked, lax.all_gather(wq_flat, 'dp', axis=0, tiled=True), prefer...]
    slice x1 -> x0, local copies, waits for them, and re-layouts: 5.76 us -> none  [body(): values = cache[..., HD:]]
    add x8 -> x0, other arithmetic: 2.54 us -> none  [the longest x3 2.37 us: combine_parts(): accum = first[2] * scale_one[..., None] + second[2] * scale_two[..., None]]
    reshape x0 -> x3, local copies, waits for them, and re-layouts: none -> 2.38 us  [the longest x1 1.34 us: body(): return result.reshape(steps, seqs, heads * HD)]
  transfers between devices with their start and end apart: 1 -> 0, of which waited for: 1 -> 0; matrix products, arithmetic and copies ran while one was open for 3% -> 0% of each run, Pallas kernels for 0% -> 0%
where the time goes in v1:
time: 38.1 us; the launch traced here: 37.9 us
  Pallas kernels  34.1 us (90%)
  local copies, waits for them, and re-layouts  3.12 us (8%)
  other arithmetic  0.64 us (2%)
    pallas_call x1, Pallas kernels, body(): pl.pallas_call(functools.partial(kernel, n, nt), out_shape=jax.ShapeDtype...  34.1 us
    reshape x1, local copies, waits for them, and re-layouts, body(): return result.reshape(steps, seqs, heads * HD)  1.34 us
    reshape x1, local copies, waits for them, and re-layouts, body(): blocks = hidden.reshape(rows, n, nt, depth)  1.03 us

profile of v1, /device:TPU:0, one launch (start us, length us, event | category | flops | bytes accessed | tf_op | source)
XLA Modules:
  0.0 37.9 jit_solution(12143341703553497692)
XLA Ops:
  0.0 0.0 copy-start
  0.0 1.0 %reshape.12 = bf16[8,8,4,256]{3,2,1,0:T(4,128)(2,1)S(1)} reshape(bf16[4,2,8192]{2,1,0:T(2,128)(2,1)} %param.6) | data formatting | bytes 262144 | tf_op jit(solution)/shard_map/reshape | solution.py:397
  1.0 0.1 constant_dynamic-slice_fusion
  1.1 0.6 %convert_bitcast_fusion.hid = f32[8,8,256]{2,1,0:T(8,128)} fusion(bf16[8,8,1,256]{3,2,1,0:T(2,128)(2,1)S(1)} %constant_dynamic-slice_fusion), kind=kLoop, calls=%fused_computation | loop fusion | flops 16384 | bytes 98304 | tf_op jit(solution)/shard_map/transpose | solution.py:399
  1.8 0.0 copy-done
  1.8 0.6 %pad.4.fresh = bf16[128,256]{1,0:T(8,128)(2,1)} pad(bf16[8,256]{1,0:T(8,128)(2,1)S(1)} %reshape.13, bf16[]{:T(256)} %constant.32.clone.1), padding=0_120x0_0 | pad | bytes 69634 | tf_op jit(solution)/shard_map/jit(_pad)/pad | solution.py:401
  2.4 34.1 %shard_map.55 = bf16[8,1024]{1,0:T(8,128)(2,1)} custom-call(s32[2]{0:T(128)} %lengths.1, f32[8,8,256]{2,1,0:T(8,128)} %convert_bitcast_fusion.hid, bf16[128,256]{1,0:T(8,128)(2,1)} %pad.4.fresh, bf16[256,4096]{1,0:T(8,128)(2,1)} %wq.1, bf16[2,4,2048,256]{3,2,1,0:T(8,128)(2,1)} %cache.1), custom_call_target="tpu_custom_call" | custom-call | tf_op jit(solution)/shard_map/pallas_call | solution.py:406
  36.5 1.3 %reshape.14 = bf16[4,2,1024]{2,1,0:T(2,128)(2,1)} reshape(bf16[8,1024]{1,0:T(8,128)(2,1)} %shard_map.55) | data formatting | bytes 32768 | tf_op jit(solution)/shard_map/reshape | solution.py:452
  (2 shorter events, 0.1 us)
Async XLA Ops:
  0.0 1.8 %copy-start = (bf16[4,2,4,256]{3,2,1,0:T(4,128)(2,1)S(1)}, bf16[4,2,4,256]{3,2,1,0:T(4,128)(2,1)}, u32[]{:S(2)}) copy-start(bf16[4,2,4,256]{3,2,1,0:T(4,128)(2,1)} %param.8) | copy-start | bytes 49156

commit v2 on v1

--- a/solution.py
+++ b/solution.py
@@ -16,15 +16,19 @@
 def kernel(
     n,
     nt,
+    blocked,
     lengths,
     hid,
-    fresh,
+    blocks,
+    new_kv,
     wq,
     cache,
     out,
     wq_own,
     wq_other,
     kv,
+    fresh,
+    x_sc,
     xg,
     yown,
     ysend,
@@ -66,9 +70,12 @@
     chip = d // 2
     chips = n // 2
     mate = d + 1 - 2 * core
-    rows = hid.shape[1]
+    steps, seqs, width = hid.shape
+    depth = wq_own.shape[0]
+    rows = steps * seqs
     half = wq_own.shape[1]
-    seqs, kvh, ctx, _ = kv.shape
+    _, kvh, ctx, _ = kv.shape
+    drains = []
     heads = QH // nt
     group = QH // kvh
     scale = 1.0 / HD**0.5
@@ -105,9 +112,15 @@
 
     pl.semaphore_wait(barrier, n - 1 + 2 * (nt - 1))
 
+    def columns_of(peer):
+        if blocked:
+            return blocks.at[peer]
+        start = pl.multiple_of((peer * nt + t) * depth, depth)
+        return hid.at[:, :, pl.ds(start, depth)]
+
     def x_copy(k, slot, peer, source):
         return pltpu.make_async_remote_copy(
-            src_ref=hid.at[peer],
+            src_ref=columns_of(peer),
             dst_ref=xg.at[slot],
             send_sem=sx_s.at[k],
             recv_sem=sx_r.at[source],
@@ -119,7 +132,11 @@
     def _(k):
         x_copy(k, d, lax.rem(d + k, n), d).start()
 
-    xg[d] = hid[d]
+    xg[d] = columns_of(d)[...]
+    for i in range(steps):
+        for s in range(seqs):
+            r = (i * seqs + s) * kvh
+            fresh[r : r + kvh, :] = new_kv[i, s].astype(jnp.float32)
     load_other.wait()
     load_own.wait()
 
@@ -128,7 +145,15 @@
         peer = lax.rem(d + k, n)
         x_copy(k, peer, peer, peer).wait_recv()
 
-    x = xg[...].reshape(n * rows, xg.shape[2]).astype(jnp.bfloat16)
+    drains.append(lambda: pl.loop(1, n)(lambda k: x_copy(k, d, lax.rem(d + k, n), d).wait_send()))
+    if blocked:
+        x = xg[...].reshape(n * rows, depth).astype(jnp.bfloat16)
+    else:
+        for p in range(n):
+            for i in range(steps):
+                r = p * rows + i * seqs
+                x_sc[r : r + seqs, :] = xg[p, i].astype(jnp.float32)
+        x = x_sc[...].astype(jnp.bfloat16)
 
     psend[...] = (
         jnp.dot(x, wq_other[...], preferred_element_type=jnp.float32)
@@ -157,6 +182,8 @@
         chips, 2 * rows, half
     )
 
+    drains.append(lambda: pl.loop(1, chips + 1)(lambda k: p_copy(order(k)).wait_send()))
+
     def y_copy(k, slot, peer, source):
         return pltpu.make_async_remote_copy(
             src_ref=ysend.at[peer],
@@ -184,6 +211,8 @@
 
     z = lax.fori_loop(1, chips, y_add, z0)
 
+    drains.append(lambda: pl.loop(1, chips)(lambda k: y_copy(k, chip, order(k), chip).wait_send()))
+
     part = half // nt
     for j in range(nt):
         zsend[j] = z[:, j * part : (j + 1) * part].astype(zsend.dtype)
@@ -211,6 +240,10 @@
     for c in range(2):
         qsend[c] = piece[c * rows : (c + 1) * rows].astype(jnp.bfloat16)
 
+    drains.append(
+        lambda: pl.loop(1, nt)(lambda k: z_copy(k, t, lax.rem(t + k, nt), t).wait_send())
+    )
+
     def q_copy(k, which, peer_core, peer, slot):
         return pltpu.make_async_remote_copy(
             src_ref=qsend.at[peer_core],
@@ -239,6 +272,16 @@
         q_copy(k, 0, core, peer, core * nt + peer).wait_recv()
         q_copy(k, 1, core, peer, (1 - core) * nt + peer).wait_recv()
 
+    def q_drain():
+        q_copy(0, 1, 1 - core, t, mine).wait_send()
+
+        @pl.loop(1, nt)
+        def _(k):
+            peer = lax.rem(t + k, nt)
+            q_copy(k, 0, core, peer, mine).wait_send()
+            q_copy(k, 1, 1 - core, peer, mine).wait_send()
+
+    drains.append(q_drain)
     heads_slot = part // HD
     for slot in range(2 * nt):
         block = qbuf[slot].astype(jnp.float32)
@@ -246,7 +289,6 @@
             h = slot * heads_slot + j
             q_sc[h * rows : (h + 1) * rows, :] = block[:, j * HD : (j + 1) * HD]
 
-    steps = rows // seqs
     band = group * rows
     position = t * ctx + lax.broadcasted_iota(jnp.int32, (1, ctx), 1)
     owned = heads * rows
@@ -314,23 +356,28 @@
 
     own = pl.ds(pl.multiple_of(t * owned, owned), owned)
     q_own = q_sc[own, :].astype(jnp.bfloat16)
+    new_keys = fresh[:, :HD].astype(jnp.bfloat16)
+    new_values = fresh[:, HD:].astype(jnp.bfloat16)
     new_scores = (
         lax.dot_general(
-            q_own, fresh[:, :HD], (((1,), (1,)), ((), ())), preferred_element_type=jnp.float32
+            q_own, new_keys, (((1,), (1,)), ((), ())), preferred_element_type=jnp.float32
         )
         * scale
     )
     row = lax.broadcasted_iota(jnp.int32, new_scores.shape, 0)
     col = lax.broadcasted_iota(jnp.int32, new_scores.shape, 1)
-    row_seq = lax.rem(row, seqs)
-    row_step = lax.rem(row, rows) // seqs
-    causal = (row_seq == lax.rem(col, seqs)) & (row_step >= col // seqs)
+    col_row = col // kvh
+    causal = (
+        (lax.rem(col, kvh) == t * heads // group)
+        & (lax.rem(row, seqs) == lax.rem(col_row, seqs))
+        & (lax.rem(row, rows) // seqs >= col_row // seqs)
+    )
     new_masked = jnp.where(causal, new_scores, NEG)
     top = jnp.max(new_masked, axis=-1, keepdims=True)
     new_weights = jnp.where(causal, jnp.exp(new_masked - top), 0.0)
     denom = jnp.sum(new_weights, axis=-1, keepdims=True)
     accum = jnp.dot(
-        new_weights.astype(jnp.bfloat16), fresh[:, HD:], preferred_element_type=jnp.float32
+        new_weights.astype(jnp.bfloat16), new_values, preferred_element_type=jnp.float32
     )
 
     def join(state, best, total, acc):
@@ -354,30 +401,20 @@
     top, denom, accum = lax.fori_loop(1, nt, a_join, state)
     result = accum / denom
     for j in range(heads):
-        out[:, j * HD : (j + 1) * HD] = result[j * rows : (j + 1) * rows].astype(out.dtype)
-
-    @pl.loop(1, n)
-    def _(k):
-        x_copy(k, d, lax.rem(d + k, n), d).wait_send()
-
-    @pl.loop(1, chips + 1)
-    def _(k):
-        p_copy(order(k)).wait_send()
-
-    @pl.loop(1, chips)
-    def _(k):
-        y_copy(k, chip, order(k), chip).wait_send()
-
-    q_copy(0, 1, 1 - core, t, mine).wait_send()
-
-    @pl.loop(1, nt)
-    def _(k):
-        peer = lax.rem(t + k, nt)
-        z_copy(k, t, peer, t).wait_send()
-        q_copy(k, 0, core, peer, mine).wait_send()
-        q_copy(k, 1, 1 - core, peer, mine).wait_send()
-        a_copy(k, t, peer, t).wait_send()
-        s_copy(k, t, peer, t).wait_send()
+        for i in range(steps):
+            r = j * rows + i * seqs
+            out[i, :, j * HD : (j + 1) * HD] = result[r : r + seqs].astype(out.dtype)
+
+    def a_drain():
+        @pl.loop(1, nt)
+        def _(k):
+            peer = lax.rem(t + k, nt)
+            a_copy(k, t, peer, t).wait_send()
+            s_copy(k, t, peer, t).wait_send()
+
+    drains.append(a_drain)
+    for drain in drains:
+        drain()
 
 
 def body(wq_flat, hidden, cache, new_kv, lengths):
@@ -391,28 +428,31 @@
     half = columns // 2
     part = half // nt
     heads = QH // nt
-    group = QH // kvh
     owned = heads * rows
     chips = n // 2
-    blocks = hidden.reshape(rows, n, nt, depth)
-    hid = lax.dynamic_index_in_dim(blocks, t, 2, keepdims=False).astype(jnp.float32)
-    hid = hid.transpose(1, 0, 2)
-    fresh = lax.dynamic_index_in_dim(new_kv, t * heads // group, 2, keepdims=False)
-    fresh = jnp.pad(fresh.reshape(rows, 2 * HD), ((0, HD - rows), (0, 0)))
     bf16, f32 = jnp.bfloat16, jnp.float32
     dma = pltpu.SemaphoreType.DMA
     vmem = pl.BlockSpec(memory_space=pltpu.VMEM)
+    blocked = depth % 128 != 0
+    blocks = hidden
+    if blocked:
+        blocks = hidden.reshape(rows, n, nt, depth)
+        blocks = lax.dynamic_index_in_dim(blocks, t, 2, keepdims=False).astype(f32)
+        blocks = blocks.transpose(1, 0, 2)
+    held = (rows, depth) if blocked else (steps, seqs, depth)
     anywhere = pl.BlockSpec(memory_space=pl.ANY)
-    result = pl.pallas_call(
-        functools.partial(kernel, n, nt),
-        out_shape=jax.ShapeDtypeStruct((rows, heads * HD), bf16),
-        in_specs=[pl.BlockSpec(memory_space=pltpu.SMEM), vmem, vmem, anywhere, anywhere],
+    return pl.pallas_call(
+        functools.partial(kernel, n, nt, blocked),
+        out_shape=jax.ShapeDtypeStruct((steps, seqs, heads * HD), bf16),
+        in_specs=[pl.BlockSpec(memory_space=pltpu.SMEM), vmem, vmem, vmem, anywhere, anywhere],
         out_specs=vmem,
         scratch_shapes=[
             pltpu.VMEM((depth, half), bf16),
             pltpu.VMEM((depth, half), bf16),
             pltpu.VMEM(cache.shape, bf16),
-            pltpu.VMEM((n, rows, depth), f32),
+            pltpu.VMEM((rows * kvh, 2 * HD), f32),
+            pltpu.VMEM((n * rows, depth), f32),
+            pltpu.VMEM((n, *held), blocks.dtype),
             pltpu.VMEM((chips, 2 * rows, half), f32),
             pltpu.VMEM((chips, 2 * rows, half), bf16),
             pltpu.VMEM((chips, 2 * rows, half), bf16),
@@ -448,8 +488,7 @@
             dma((nt,)),
         ],
         compiler_params=pltpu.CompilerParams(collective_id=0, has_side_effects=True),
-    )(lengths, hid, fresh, wq_flat, cache)
-    return result.reshape(steps, seqs, heads * HD)
+    )(lengths, hidden, blocks, new_kv, wq_flat, cache)
 
 
 def solution(mesh):

time: 38.1 us -> 35.7 us (0.937)
  local copies, waits for them, and re-layouts: 3.12 us -> 1.34 us
  other arithmetic: 0.64 us -> 0 us
    reshape x3 -> x0, local copies, waits for them, and re-layouts: 2.38 us -> none  [the longest x1 1.34 us: body(): return result.reshape(steps, seqs, heads * HD)]
    unnamed x2 -> x1, local copies, waits for them, and re-layouts: 0.01 us -> 1.34 us
    transpose x1 -> x0, other arithmetic: 0.64 us -> none  [body(): hid = hid.transpose(1, 0, 2)]
    pad x1 -> x0, local copies, waits for them, and re-layouts: 0.63 us -> none  [body(): fresh = jnp.pad(fresh.reshape(rows, 2 * HD), ((0, HD - rows), (0, 0)))]
where the time goes in v2:
time: 35.7 us; the launch traced here: 35.4 us
  Pallas kernels  34.1 us (96%)
  local copies, waits for them, and re-layouts  1.34 us (4%)
    pallas_call x1, Pallas kernels, body(): pl.pallas_call(functools.partial(kernel, n, nt, blocked), out_shape=jax.S...  34.1 us
    unnamed x1, local copies, waits for them, and re-layouts  1.34 us

profile of v2, /device:TPU:0, one launch (start us, length us, event | category | flops | bytes accessed | tf_op | source)
XLA Modules:
  0.0 35.4 jit_solution(7688422484804303766)
XLA Ops:
  0.0 34.1 %shard_map.55 = bf16[4,2,1024]{2,1,0:T(2,128)(2,1)} custom-call(s32[2]{0:T(128)} %lengths.1, bf16[4,2,8192]{2,1,0:T(2,128)(2,1)} %blocks.1, bf16[4,2,8192]{2,1,0:T(2,128)(2,1)} %blocks.1, bf16[4,2,4,256]{3,2,1,0:T(4,128)(2,1)} %new_kv.1, bf16[256,4096]{1,0:T(8,128)(2,1)} %wq.1, bf16[2,4,2048,256]{3,2,1,0:T(8,128)(2,1)} %cache.1), custom_call_target="tpu_custom_call" | custom-call | tf_op jit(solution)/shard_map/pallas_call | solution.py:444
  34.1 1.3 %copy.7 = bf16[4,2,1024]{2,1,0:T(2,128)(2,1)} copy(bf16[4,2,1024]{2,1,0:T(2,128)(2,1)} %shard_map.55) | data formatting | bytes 32768

commit v3 on v2

v3 whole, which is shorter than its diff:
```python
import functools

import jax
import jax.numpy as jnp
from jax import lax
from jax.experimental import pallas as pl
from jax.experimental.pallas import tpu as pltpu
from jax.sharding import PartitionSpec as P

QH = 32
HD = 128
MESH = pl.DeviceIdType.MESH
NEG = -1e30


def kernel(
    n,
    nt,
    blocked,
    lengths,
    hid_any,
    blocks,
    new_any,
    wq,
    cache,
    out,
    hid,
    new_kv,
    sem_in,
    wq_own,
    wq_other,
    kv,
    fresh,
    x_sc,
    xg,
    yown,
    ysend,
    yrecv,
    psend,
    precv,
    zsend,
    zrecv,
    qsend,
    qbuf,
    q_sc,
    acc_sc,
    asend,
    arecv,
    m_sc,
    l_sc,
    ssend,
    srecv,
    sem_w,
    sem_kv,
    sx_s,
    sx_r,
    sy_s,
    sy_r,
    sp_s,
    sp_r,
    sz_s,
    sz_r,
    sq_s,
    sq_r,
    sa_s,
    sa_r,
    ss_s,
    ss_r,
):
    d = lax.axis_index("dp")
    t = lax.axis_index("tensor")
    core = lax.rem(d, 2)
    chip = d // 2
    chips = n // 2
    mate = d + 1 - 2 * core
    steps, seqs, width = hid.shape
    depth = wq_own.shape[0]
    rows = steps * seqs
    half = wq_own.shape[1]
    _, kvh, ctx, _ = kv.shape
    drains = []
    heads = QH // nt
    group = QH // kvh
    scale = 1.0 / HD**0.5

    load_hid = pltpu.make_async_copy(hid_any, hid, sem_in.at[0])
    load_new = pltpu.make_async_copy(new_any, new_kv, sem_in.at[1])
    load_hid.start()
    load_new.start()
    load_other = pltpu.make_async_copy(
        wq.at[:, pl.ds(pl.multiple_of((1 - core) * half, half), half)], wq_other, sem_w.at[0]
    )
    load_own = pltpu.make_async_copy(
        wq.at[:, pl.ds(pl.multiple_of(core * half, half), half)], wq_own, sem_w.at[1]
    )
    load_other.start()
    load_own.start()
    load_kv = [
        [pltpu.make_async_copy(cache.at[s, g], kv.at[s, g], sem_kv.at[s, g]) for g in range(kvh)]
        for s in range(seqs)
    ]
    for g in range(kvh):
        for s in range(seqs):
            load_kv[s][g].start()

    barrier = pltpu.get_barrier_semaphore()

    @pl.loop(1, n)
    def _(k):
        pl.semaphore_signal(
            barrier, inc=1, device_id=(lax.rem(d + k, n), t), device_id_type=MESH
        )

    @pl.loop(1, nt)
    def _(k):
        peer = lax.rem(t + k, nt)
        pl.semaphore_signal(barrier, inc=1, device_id=(d, peer), device_id_type=MESH)
        pl.semaphore_signal(barrier, inc=1, device_id=(mate, peer), device_id_type=MESH)

    pl.semaphore_wait(barrier, n - 1 + 2 * (nt - 1))

    load_hid.wait()
    load_new.wait()

    def columns_of(peer):
        if blocked:
            return blocks.at[peer]
        start = pl.multiple_of((peer * nt + t) * depth, depth)
        return hid.at[:, :, pl.ds(start, depth)]

    def x_copy(k, slot, peer, source):
        return pltpu.make_async_remote_copy(
            src_ref=columns_of(peer),
            dst_ref=xg.at[slot],
            send_sem=sx_s.at[k],
            recv_sem=sx_r.at[source],
            device_id=(peer, t),
            device_id_type=MESH,
        )

    @pl.loop(1, n)
    def _(k):
        x_copy(k, d, lax.rem(d + k, n), d).start()

    xg[d] = columns_of(d)[...]
    for i in range(steps):
        for s in range(seqs):
            r = (i * seqs + s) * kvh
            fresh[r : r + kvh, :] = new_kv[i, s].astype(jnp.float32)
    load_other.wait()
    load_own.wait()

    @pl.loop(1, n)
    def _(k):
        peer = lax.rem(d + k, n)
        x_copy(k, peer, peer, peer).wait_recv()

    drains.append(lambda: pl.loop(1, n)(lambda k: x_copy(k, d, lax.rem(d + k, n), d).wait_send()))
    if blocked:
        x = xg[...].reshape(n * rows, depth).astype(jnp.bfloat16)
    else:
        for p in range(n):
            for i in range(steps):
                r = p * rows + i * seqs
                x_sc[r : r + seqs, :] = xg[p, i].astype(jnp.float32)
        x = x_sc[...].astype(jnp.bfloat16)

    cuts = psend.shape[0]
    wide = half // cuts

    def p_copy(c, p):
        return pltpu.make_async_remote_copy(
            src_ref=psend.at[c, p],
            dst_ref=precv.at[c, p],
            send_sem=sp_s.at[c, p],
            recv_sem=sp_r.at[c, p],
            device_id=(mate, t),
            device_id_type=MESH,
        )

    def order(k):
        return lax.rem(chip + chips - k, chips)

    for c in range(cuts):
        psend[c] = (
            jnp.dot(
                x, wq_other[:, c * wide : (c + 1) * wide], preferred_element_type=jnp.float32
            )
            .astype(jnp.bfloat16)
            .reshape(chips, 2 * rows, wide)
        )

        @pl.loop(1, chips + 1)
        def _(k):
            p_copy(c, order(k)).start()

    for c in range(cuts):
        yown[c] = jnp.dot(
            x, wq_own[:, c * wide : (c + 1) * wide], preferred_element_type=jnp.float32
        ).reshape(chips, 2 * rows, wide)

    def p_drain():
        for c in range(cuts):
            pl.loop(1, chips + 1)(lambda k: p_copy(c, order(k)).wait_send())

    drains.append(p_drain)

    def y_copy(c, k, slot, peer, source):
        return pltpu.make_async_remote_copy(
            src_ref=ysend.at[c, peer],
            dst_ref=yrecv.at[c, slot],
            send_sem=sy_s.at[c, k],
            recv_sem=sy_r.at[c, source],
            device_id=(2 * peer + core, t),
            device_id_type=MESH,
        )

    for c in range(cuts):

        @pl.loop(1, chips)
        def _(k):
            p = order(k)
            p_copy(c, p).wait_recv()
            ysend[c, p] = (yown[c, p] + precv[c, p].astype(jnp.float32)).astype(jnp.bfloat16)
            y_copy(c, k, chip, p, chip).start()

        p_copy(c, chip).wait_recv()

    part = wide // nt

    def z_copy(c, k, slot, peer, source):
        return pltpu.make_async_remote_copy(
            src_ref=zsend.at[c, peer],
            dst_ref=zrecv.at[c, slot],
            send_sem=sz_s.at[c, k],
            recv_sem=sz_r.at[c, source],
            device_id=(d, peer),
            device_id_type=MESH,
        )

    for c in range(cuts):

        def y_add(k, z):
            p = order(k)
            y_copy(c, k, p, p, p).wait_recv()
            return z + yrecv[c, p].astype(jnp.float32)

        z = lax.fori_loop(1, chips, y_add, yown[c, chip] + precv[c, chip].astype(jnp.float32))
        for j in range(nt):
            zsend[c, j] = z[:, j * part : (j + 1) * part].astype(zsend.dtype)

        @pl.loop(1, nt)
        def _(k):
            z_copy(c, k, t, lax.rem(t + k, nt), t).start()

    def yz_drain():
        for c in range(cuts):
            pl.loop(1, chips)(lambda k: y_copy(c, k, chip, order(k), chip).wait_send())
            pl.loop(1, nt)(lambda k: z_copy(c, k, t, lax.rem(t + k, nt), t).wait_send())

    drains.append(yz_drain)

    def q_copy(c, k, which, peer_core, peer, slot):
        return pltpu.make_async_remote_copy(
            src_ref=qsend.at[c, peer_core],
            dst_ref=qbuf.at[c, slot],
            send_sem=sq_s.at[c, k, which],
            recv_sem=sq_r.at[c, slot],
            device_id=(2 * chip + peer_core, peer),
            device_id_type=MESH,
        )

    mine = core * nt + t
    for c in range(cuts):

        def z_add(k, total):
            peer = lax.rem(t + k, nt)
            z_copy(c, k, peer, peer, peer).wait_recv()
            return total + zrecv[c, peer].astype(jnp.float32)

        piece = lax.fori_loop(1, nt, z_add, zsend[c, t].astype(jnp.float32))
        for i in range(2):
            qsend[c, i] = piece[i * rows : (i + 1) * rows].astype(jnp.bfloat16)

        @pl.loop(1, nt)
        def _(k):
            peer = lax.rem(t + k, nt)
            q_copy(c, k, 0, core, peer, mine).start()
            q_copy(c, k, 1, 1 - core, peer, mine).start()

        q_copy(c, 0, 1, 1 - core, t, mine).start()
        qbuf[c, mine] = qsend[c, core]

    def q_drain():
        for c in range(cuts):
            q_copy(c, 0, 1, 1 - core, t, mine).wait_send()

            @pl.loop(1, nt)
            def _(k):
                peer = lax.rem(t + k, nt)
                q_copy(c, k, 0, core, peer, mine).wait_send()
                q_copy(c, k, 1, 1 - core, peer, mine).wait_send()

    drains.append(q_drain)

    band = group * rows
    position = t * ctx + lax.broadcasted_iota(jnp.int32, (1, ctx), 1)
    owned = heads * rows
    eye = lax.broadcasted_iota(jnp.int32, (owned, HD), 0) == lax.broadcasted_iota(
        jnp.int32, (owned, HD), 1
    )

    def a_copy(slot, peer, source):
        return pltpu.make_async_remote_copy(
            src_ref=asend.at[peer],
            dst_ref=arecv.at[slot],
            send_sem=sa_s.at[peer],
            recv_sem=sa_r.at[source],
            device_id=(d, peer),
            device_id_type=MESH,
        )

    def s_copy(slot, peer, source):
        return pltpu.make_async_remote_copy(
            src_ref=ssend.at[peer],
            dst_ref=srecv.at[slot],
            send_sem=ss_s.at[peer],
            recv_sem=ss_r.at[source],
            device_id=(d, peer),
            device_id_type=MESH,
        )

    def attend(g, s):
        span = pl.ds(g * band + s, group * steps, stride=seqs)
        q = q_sc[span, :].astype(jnp.bfloat16)
        scores = lax.dot_general(
            q, kv[s, g, :, :HD], (((1,), (1,)), ((), ())), preferred_element_type=jnp.float32
        )
        masked = jnp.where(position < lengths[s], scores * scale, NEG)
        best = jnp.max(masked, axis=-1, keepdims=True)
        weights = jnp.exp(masked - best)
        total = jnp.sum(weights, axis=-1, keepdims=True)
        acc = jnp.dot(
            weights.astype(jnp.bfloat16), kv[s, g, :, HD:], preferred_element_type=jnp.float32
        )
        acc_sc[span, :] = acc
        m_sc[span, :] = jnp.broadcast_to(best, acc.shape)
        l_sc[span, :] = jnp.broadcast_to(total, acc.shape)

    heads_slot = part // HD
    side = kvh // 2 // cuts
    finished = set()
    sent = set()
    for c in range(cuts):
        q_copy(c, 0, 1, 1 - core, t, (1 - core) * nt + t).wait_recv()

        @pl.loop(1, nt)
        def _(k):
            peer = lax.rem(t + k, nt)
            q_copy(c, k, 0, core, peer, core * nt + peer).wait_recv()
            q_copy(c, k, 1, core, peer, (1 - core) * nt + peer).wait_recv()

        for slot in range(2 * nt):
            block = qbuf[c, slot].astype(jnp.float32)
            first = (slot // nt * half + c * wide) // HD + slot % nt * heads_slot
            for j in range(heads_slot):
                h = first + j
                q_sc[h * rows : (h + 1) * rows, :] = block[:, j * HD : (j + 1) * HD]

        ready = [i * (kvh // 2) + c * side + j for i in range(2) for j in range(side)]
        for g in ready:
            for s in range(seqs):
                load_kv[s][g].wait()
        for g in ready:
            for s in range(seqs):
                attend(g, s)
        finished.update(ready)
        for j in range(nt):
            needs = {h // group for h in range(j * heads, (j + 1) * heads)}
            if j in sent or not needs <= finished:
                continue
            sent.add(j)
            window = slice(j * owned, (j + 1) * owned)
            asend[j] = acc_sc[window, :].astype(asend.dtype)
            for i, ref in enumerate((m_sc, l_sc)):
                ssend[j, i : i + 1, :] = jnp.sum(
                    jnp.where(eye, ref[window, :], 0.0), axis=0, keepdims=True
                )

            @pl.when(t != j)
            def _():
                a_copy(t, j, t).start()
                s_copy(t, j, t).start()

    own = pl.ds(pl.multiple_of(t * owned, owned), owned)
    q_own = q_sc[own, :].astype(jnp.bfloat16)
    new_keys = fresh[:, :HD].astype(jnp.bfloat16)
    new_values = fresh[:, HD:].astype(jnp.bfloat16)
    new_scores = (
        lax.dot_general(
            q_own, new_keys, (((1,), (1,)), ((), ())), preferred_element_type=jnp.float32
        )
        * scale
    )
    row = lax.broadcasted_iota(jnp.int32, new_scores.shape, 0)
    col = lax.broadcasted_iota(jnp.int32, new_scores.shape, 1)
    col_row = col // kvh
    causal = (
        (lax.rem(col, kvh) == t * heads // group)
        & (lax.rem(row, seqs) == lax.rem(col_row, seqs))
        & (lax.rem(row, rows) // seqs >= col_row // seqs)
    )
    new_masked = jnp.where(causal, new_scores, NEG)
    top = jnp.max(new_masked, axis=-1, keepdims=True)
    new_weights = jnp.where(causal, jnp.exp(new_masked - top), 0.0)
    denom = jnp.sum(new_weights, axis=-1, keepdims=True)
    accum = jnp.dot(
        new_weights.astype(jnp.bfloat16), new_values, preferred_element_type=jnp.float32
    )

    def join(state, best, total, acc):
        top, denom, accum = state
        peak = jnp.maximum(top, best)
        left = jnp.exp(top - peak)
        right = jnp.exp(best - peak)
        return peak, denom * left + total * right, accum * left + acc * right

    state = join((top, denom, accum), m_sc[own, :][:, :1], l_sc[own, :][:, :1], acc_sc[own, :])

    def a_join(k, state):
        peer = lax.rem(t + k, nt)
        a_copy(peer, peer, peer).wait_recv()
        s_copy(peer, peer, peer).wait_recv()
        stats = srecv[peer]
        best = jnp.sum(jnp.where(eye, stats[0:1, :], 0.0), axis=1, keepdims=True)
        total = jnp.sum(jnp.where(eye, stats[1:2, :], 0.0), axis=1, keepdims=True)
        return join(state, best, total, arecv[peer].astype(jnp.float32))

    top, denom, accum = lax.fori_loop(1, nt, a_join, state)
    result = accum / denom
    for j in range(heads):
        for i in range(steps):
            r = j * rows + i * seqs
            out[i, :, j * HD : (j + 1) * HD] = result[r : r + seqs].astype(out.dtype)

    def a_drain():
        @pl.loop(1, nt)
        def _(k):
            peer = lax.rem(t + k, nt)
            a_copy(t, peer, t).wait_send()
            s_copy(t, peer, t).wait_send()

    drains.append(a_drain)
    for drain in drains:
        drain()


def body(wq_flat, hidden, cache, new_kv, lengths):
    nt = lax.axis_size("tensor")
    n = lax.axis_size("dp")
    t = lax.axis_index("tensor")
    steps, seqs, width = hidden.shape
    rows = steps * seqs
    depth, columns = wq_flat.shape
    kvh, ctx = cache.shape[1], cache.shape[2]
    half = columns // 2
    cuts = 2 if half // (2 * nt) % HD == 0 and kvh % 4 == 0 else 1
    wide = half // cuts
    part = wide // nt
    heads = QH // nt
    owned = heads * rows
    chips = n // 2
    bf16, f32 = jnp.bfloat16, jnp.float32
    dma = pltpu.SemaphoreType.DMA
    vmem = pl.BlockSpec(memory_space=pltpu.VMEM)
    blocked = depth % 128 != 0
    blocks = hidden
    if blocked:
        blocks = hidden.reshape(rows, n, nt, depth)
        blocks = lax.dynamic_index_in_dim(blocks, t, 2, keepdims=False).astype(f32)
        blocks = blocks.transpose(1, 0, 2)
    held = (rows, depth) if blocked else (steps, seqs, depth)
    anywhere = pl.BlockSpec(memory_space=pl.ANY)
    result = pl.pallas_call(
        functools.partial(kernel, n, nt, blocked),
        out_shape=jax.ShapeDtypeStruct((steps, seqs, heads * HD), f32),
        in_specs=[pl.BlockSpec(memory_space=pltpu.SMEM), anywhere, vmem if blocked else anywhere, anywhere, anywhere, anywhere],
        out_specs=vmem,
        scratch_shapes=[
            pltpu.VMEM(hidden.shape, bf16),
            pltpu.VMEM(new_kv.shape, bf16),
            dma((2,)),
            pltpu.VMEM((depth, half), bf16),
            pltpu.VMEM((depth, half), bf16),
            pltpu.VMEM(cache.shape, bf16),
            pltpu.VMEM((rows * kvh, 2 * HD), f32),
            pltpu.VMEM((n * rows, depth), f32),
            pltpu.VMEM((n, *held), blocks.dtype),
            pltpu.VMEM((cuts, chips, 2 * rows, wide), f32),
            pltpu.VMEM((cuts, chips, 2 * rows, wide), bf16),
            pltpu.VMEM((cuts, chips, 2 * rows, wide), bf16),
            pltpu.VMEM((cuts, chips, 2 * rows, wide), bf16),
            pltpu.VMEM((cuts, chips, 2 * rows, wide), bf16),
            pltpu.VMEM((cuts, nt, 2 * rows, part), bf16),
            pltpu.VMEM((cuts, nt, 2 * rows, part), bf16),
            pltpu.VMEM((cuts, 2, rows, part), bf16),
            pltpu.VMEM((cuts, 2 * nt, rows, part), bf16),
            pltpu.VMEM((QH * rows, HD), f32),
            pltpu.VMEM((QH * rows, HD), f32),
            pltpu.VMEM((nt, owned, HD), bf16),
            pltpu.VMEM((nt, owned, HD), bf16),
            pltpu.VMEM((QH * rows, HD), f32),
            pltpu.VMEM((QH * rows, HD), f32),
            pltpu.VMEM((nt, 8, HD), f32),
            pltpu.VMEM((nt, 8, HD), f32),
            dma((2,)),
            dma((seqs, kvh)),
            dma((n,)),
            dma((n,)),
            dma((cuts, chips)),
            dma((cuts, chips)),
            dma((cuts, chips)),
            dma((cuts, chips)),
            dma((cuts, nt)),
            dma((cuts, nt)),
            dma((cuts, nt, 2)),
            dma((cuts, 2 * nt)),
            dma((nt,)),
            dma((nt,)),
            dma((nt,)),
            dma((nt,)),
        ],
        compiler_params=pltpu.CompilerParams(collective_id=0, has_side_effects=True),
    )(lengths, hidden, blocks, new_kv, wq_flat, cache)
    return result.astype(bf16)


def solution(mesh):
    placed = (
        P(("dp", "tensor"), None),
        P(None, "dp", None),
        P("dp", None, "tensor", None),
        P(None, "dp", None, None),
        P("dp"),
    )
    return jax.shard_map(
        body, mesh=mesh, in_specs=placed, out_specs=P(None, "dp", "tensor"), check_vma=False
    )
```

time: 35.7 us -> 32.4 us (0.908)
  Pallas kernels: 34.1 us -> 30.8 us
  other arithmetic: 0 us -> 1.38 us
  local copies, waits for them, and re-layouts: 1.34 us -> 0 us
    pallas_call x1, Pallas kernels: 34.1 us -> 30.8 us  [body(): pl.pallas_call(functools.partial(kernel, n, nt, blocked), out_shape=jax.S...]
    convert_element_type x0 -> x1, other arithmetic: none -> 1.38 us  [body(): return result.astype(bf16)]
    unnamed x1 -> x0, local copies, waits for them, and re-layouts: 1.34 us -> none
where the time goes in v3:
time: 32.4 us; the launch traced here: 32.2 us
  Pallas kernels  30.8 us (95%)
  other arithmetic  1.38 us (4%)
    pallas_call x1, Pallas kernels, body(): pl.pallas_call(functools.partial(kernel, n, nt, blocked), out_shape=jax.S...  30.8 us
    convert_element_type x1, other arithmetic, body(): return result.astype(bf16)  1.38 us

profile of v3, /device:TPU:0, one launch (start us, length us, event | category | flops | bytes accessed | tf_op | source)
XLA Modules:
  0.0 32.2 jit_solution(13736521659735210394)
XLA Ops:
  0.0 30.8 %shard_map.55 = f32[4,2,1024]{2,1,0:T(2,128)} custom-call(s32[2]{0:T(128)} %lengths.1, bf16[4,2,8192]{2,1,0:T(2,128)(2,1)} %blocks.1, bf16[4,2,8192]{2,1,0:T(2,128)(2,1)} %blocks.1, bf16[4,2,4,256]{3,2,1,0:T(4,128)(2,1)} %new_any.1, bf16[256,4096]{1,0:T(8,128)(2,1)} %wq.1, bf16[2,4,2048,256]{3,2,1,0:T(8,128)(2,1)} %cache.1), custom_call_target="tpu_custom_call" | custom-call | tf_op jit(solution)/shard_map/pallas_call | solution.py:484
  30.8 1.4 %convert_element_type.3 = bf16[4,2,1024]{2,1,0:T(2,128)(2,1)} convert(f32[4,2,1024]{2,1,0:T(2,128)} %shard_map.55) | non-fusion elementwise | flops 8192 | bytes 49152 | tf_op jit(solution)/shard_map/convert_element_type | solution.py:535

commit v4 on v3

--- a/solution.py
+++ b/solution.py
@@ -331,8 +331,9 @@
         )
 
     def attend(g, s):
-        span = pl.ds(g * band + s, group * steps, stride=seqs)
-        q = q_sc[span, :].astype(jnp.bfloat16)
+        base = pl.ds(pl.multiple_of(g * band, band), band)
+        span = pl.ds(s, group * steps, stride=seqs)
+        q = q_sc.at[base][span, :].astype(jnp.bfloat16)
         scores = lax.dot_general(
             q, kv[s, g, :, :HD], (((1,), (1,)), ((), ())), preferred_element_type=jnp.float32
         )
@@ -343,14 +344,14 @@
         acc = jnp.dot(
             weights.astype(jnp.bfloat16), kv[s, g, :, HD:], preferred_element_type=jnp.float32
         )
-        acc_sc[span, :] = acc
-        m_sc[span, :] = jnp.broadcast_to(best, acc.shape)
-        l_sc[span, :] = jnp.broadcast_to(total, acc.shape)
+        acc_sc.at[base][span, :] = acc
+        m_sc.at[base][span, :] = jnp.broadcast_to(best, acc.shape)
+        l_sc.at[base][span, :] = jnp.broadcast_to(total, acc.shape)
 
     heads_slot = part // HD
     side = kvh // 2 // cuts
-    finished = set()
-    sent = set()
+    per = group // heads
+    far = (2 * t < nt).astype(jnp.int32)
     for c in range(cuts):
         q_copy(c, 0, 1, 1 - core, t, (1 - core) * nt + t).wait_recv()
 
@@ -371,26 +372,23 @@
         for g in ready:
             for s in range(seqs):
                 load_kv[s][g].wait()
-        for g in ready:
+        for low, high in zip(ready, ready[::-1]):
+            g = low + (high - low) * far
             for s in range(seqs):
                 attend(g, s)
-        finished.update(ready)
-        for j in range(nt):
-            needs = {h // group for h in range(j * heads, (j + 1) * heads)}
-            if j in sent or not needs <= finished:
-                continue
-            sent.add(j)
-            window = slice(j * owned, (j + 1) * owned)
-            asend[j] = acc_sc[window, :].astype(asend.dtype)
-            for i, ref in enumerate((m_sc, l_sc)):
-                ssend[j, i : i + 1, :] = jnp.sum(
-                    jnp.where(eye, ref[window, :], 0.0), axis=0, keepdims=True
-                )
-
-            @pl.when(t != j)
-            def _():
-                a_copy(t, j, t).start()
-                s_copy(t, j, t).start()
+            for i in range(per):
+                j = g * per + i
+                window = pl.ds(pl.multiple_of(j * owned, owned), owned)
+                asend[j] = acc_sc[window, :].astype(asend.dtype)
+                for at, ref in enumerate((m_sc, l_sc)):
+                    ssend[j, at : at + 1, :] = jnp.sum(
+                        jnp.where(eye, ref[window, :], 0.0), axis=0, keepdims=True
+                    )
+
+                @pl.when(t != j)
+                def _():
+                    a_copy(t, j, t).start()
+                    s_copy(t, j, t).start()
 
     own = pl.ds(pl.multiple_of(t * owned, owned), owned)
     q_own = q_sc[own, :].astype(jnp.bfloat16)
@@ -483,7 +481,7 @@
     anywhere = pl.BlockSpec(memory_space=pl.ANY)
     result = pl.pallas_call(
         functools.partial(kernel, n, nt, blocked),
-        out_shape=jax.ShapeDtypeStruct((steps, seqs, heads * HD), f32),
+        out_shape=pltpu.VMEM((steps, seqs, heads * HD), f32),
         in_specs=[pl.BlockSpec(memory_space=pltpu.SMEM), anywhere, vmem if blocked else anywhere, anywhere, anywhere, anywhere],
         out_specs=vmem,
         scratch_shapes=[

time: 32.4 us -> 30.1 us (0.929)
  Pallas kernels: 30.8 us -> 29.3 us
  other arithmetic: 1.38 us -> 0.62 us
    pallas_call x1, Pallas kernels: 30.8 us -> 29.3 us  [body(): pl.pallas_call(functools.partial(kernel, n, nt, blocked), out_shape=pltpu...]
    convert_element_type x1, other arithmetic: 1.38 us -> 0.62 us  [body(): return result.astype(bf16)]
where the time goes in v4:
time: 30.1 us; the launch traced here: 29.9 us
  Pallas kernels  29.3 us (97%)
  other arithmetic  0.62 us (2%)
    pallas_call x1, Pallas kernels, body(): pl.pallas_call(functools.partial(kernel, n, nt, blocked), out_shape=pltpu...  29.3 us
    convert_element_type x1, other arithmetic, body(): return result.astype(bf16)  0.62 us

profile of v4, /device:TPU:0, one launch (start us, length us, event | category | flops | bytes accessed | tf_op | source)
XLA Modules:
  0.0 29.9 jit_solution(11105400480523567952)
XLA Ops:
  0.0 29.3 %shard_map.55 = f32[4,2,1024]{2,1,0:T(2,128)S(1)} custom-call(s32[2]{0:T(128)} %lengths.1, bf16[4,2,8192]{2,1,0:T(2,128)(2,1)} %blocks.1, bf16[4,2,8192]{2,1,0:T(2,128)(2,1)} %blocks.1, bf16[4,2,4,256]{3,2,1,0:T(4,128)(2,1)} %new_any.1, bf16[256,4096]{1,0:T(8,128)(2,1)} %wq.1, bf16[2,4,2048,256]{3,2,1,0:T(8,128)(2,1)} %cache.1), custom_call_target="tpu_custom_call" | custom-call | tf_op jit(solution)/shard_map/pallas_call | solution.py:482
  29.3 0.6 %convert_element_type.3 = bf16[4,2,1024]{2,1,0:T(2,128)(2,1)} convert(f32[4,2,1024]{2,1,0:T(2,128)S(1)} %shard_map.55) | non-fusion elementwise | flops 8192 | bytes 49152 | tf_op jit(solution)/shard_map/convert_element_type | solution.py:533
